TPU v7x, 256 devices: a whole 4x4x8 slice. The times are simulated.
256 devices in a mesh: dom: 32 (over x, z), load: 8 (over y, core).
Axes of the slice: x: 4, y: 4, z: 8, core: 2. Of those that a mesh axis runs over, the one named last changes fastest.
Arguments:
- load_current: float32 [8, 49152], P('load', 'dom'), may hold values from 0.1 to 1
- worst_node: int32 [8], P('load'), may hold values from 0 to 49151
- cond_diag: float32 [49152], P('dom'), may hold values from 0.5 to 4
- branch: float32 [384, 128, 128], P('dom'), may hold values from -0.5 to 0.5
- precond_factor: float32 [384, 128, 128], P('dom'), may hold values from -0.5 to 0.5
- coupling: float32 [5, 384, 128, 128], P(None, 'dom'), may hold values from -0.5 to 0.5
- sep_map: int32 [5, 384], P(None, 'dom'), may hold values from 0 to 11
- strap_ends: int32 [2, 524288], P(None, 'dom'), may hold values from 0 to 1535
Outputs:
- voltages: float32 [2, 8, 49152], P(None, 'load', 'dom')
- strap_grad: float32 [524288], P('dom')
Inputs may be any that keep to these rules, and one draw needn't show every extreme that they name: `sep_map`: each entry names an interior block of the same partition as the separator block. `strap_ends`: both ends of a strap lie in the partition that holds the strap. `worst_node`: a global node index.
All inputs are finite; a program needn't handle non-finite values.
Results may differ from a plain program's by a relative error of at most 0.00017.
Values sent between devices are 32-bit elements; how exact they have to be, the bound alone decides.
No kernel may reach another device: no remote copies, remote signals or barrier semaphores. Data moves between devices by JAX's collectives and lax.ppermute only.
A program may use at most 128 MiB of HBM per device.

v0:
```python
import math
import jax
import jax.numpy as jnp
from jax import lax
from jax.sharding import PartitionSpec as P

ITERS = 4
HIGHEST = lax.Precision.HIGHEST


def swapped(value, axis, apart):
    mask = 2**apart
    pairs = [(source, source ^ mask) for source in range(lax.axis_size(axis))]
    return lax.ppermute(value, axis, pairs)


def subtree_sums(contrib):
    levels = contrib.shape[0]
    finished = []
    pending = contrib
    for level_no in range(levels):
        pending = pending + swapped(pending, "dom", level_no)
        finished.append(pending[0])
        pending = pending[1:]
    return jnp.stack(finished)


def coarse_part(blocks, coupling, picker, level_weights):
    selected = jnp.einsum("ljb,rbn->lrjn", picker, blocks, precision=HIGHEST)
    contrib = jnp.einsum("ljmn,lrjn->lrjm", coupling, selected, precision=HIGHEST)
    group_sums = subtree_sums(contrib)
    returned = jnp.einsum("ljmn,lrjm->lrjn", coupling, group_sums, precision=HIGHEST)
    weighted = picker * level_weights[:, None, None]
    return jnp.einsum("ljb,lrjn->rbn", weighted, returned, precision=HIGHEST)


def factor_apply(factor, blocks):
    inner = jnp.einsum("jnk,rjn->rjk", factor, blocks, precision=HIGHEST)
    return jnp.einsum("jnk,rjk->rjn", factor, inner, precision=HIGHEST)


def column_sums(first, second):
    return lax.psum(jnp.sum(first * second, axis=(1, 2)), "dom")


def shards(
    load_current, worst_node, cond_diag, branch, precond_factor, coupling, sep_map, strap_ends
):
    levels = coupling.shape[0]
    nblocks = branch.shape[0]
    width = branch.shape[1]
    node_count = nblocks * width
    time_count = load_current.shape[0]
    shunt = cond_diag.reshape(nblocks, width)
    picker = (sep_map[:, :, None] == jnp.arange(nblocks, dtype=jnp.int32)[None, None, :]).astype(
        jnp.float32
    )
    op_weights = jnp.array(
        [1.0 / math.sqrt(2.0 ** (level_no + 1)) for level_no in range(levels)], jnp.float32
    )
    pre_weights = 0.5 * op_weights
    node_ids = lax.axis_index("dom") * node_count + jnp.arange(node_count, dtype=jnp.int32)
    adjoint_rhs = (node_ids[None, :] == worst_node[:, None]).astype(jnp.float32)
    sources = jnp.concatenate([load_current, adjoint_rhs], 0).reshape(
        2 * time_count, nblocks, width
    )

    def apply_precond(blocks):
        return (
            blocks / (shunt + 1.0)
            + 0.25 * factor_apply(precond_factor, blocks)
            + coarse_part(blocks, coupling, picker, pre_weights)
        )

    solution = jnp.zeros_like(sources)
    residual = sources
    precond_res = apply_precond(residual)
    rho_now = column_sums(residual, precond_res)
    direction = precond_res
    for iteration in range(ITERS):
        mapped = (
            shunt * direction
            + factor_apply(branch, direction)
            + coarse_part(direction, coupling, picker, op_weights)
        )
        step_size = rho_now / column_sums(direction, mapped)
        solution = solution + step_size[:, None, None] * direction
        residual = residual - step_size[:, None, None] * mapped
        if iteration + 1 < ITERS:
            precond_res = apply_precond(residual)
            rho_new = column_sums(residual, precond_res)
            direction = precond_res + (rho_new / rho_now)[:, None, None] * direction
            rho_now = rho_new
    voltages = solution.reshape(2, time_count, node_count)
    forward = voltages[0]
    adjoint = voltages[1]
    drop_diff = forward[:, strap_ends[0]] - forward[:, strap_ends[1]]
    adj_diff = adjoint[:, strap_ends[0]] - adjoint[:, strap_ends[1]]
    strap_grad = lax.psum(-jnp.sum(adj_diff * drop_diff, axis=0), "load")
    return (voltages, strap_grad)


def solution(mesh):
    placed = (
        P("load", "dom"),
        P("load"),
        P("dom"),
        P("dom", None, None),
        P("dom", None, None),
        P(None, "dom", None, None),
        P(None, "dom"),
        P(None, "dom"),
    )
    return jax.shard_map(
        shards,
        mesh=mesh,
        in_specs=placed,
        out_specs=(P(None, "load", "dom"), P("dom")),
        check_vma=False,
    )
```

profile of v0, /device:TPU:2, one launch (start us, length us, event | category | flops | bytes accessed | tf_op | source)
XLA Modules:
  0.0 1265.0 jit_solution(7190926894018627140)
XLA Ops:
  10.0 7.9 convolution_bitcast_fusion.7
  27.7 7.0 collective-permute-start.2
  51.4 6.2 convolution_bitcast_fusion.6
  67.1 6.9 collective-permute-start.7
  90.7 64.4 %all-reduce = (f32[2]{0:T(128)S(1)}, f32[2]{0:T(128)S(1)}) all-reduce(f32[2]{0:T(128)S(1)} %get-tuple-element.7, f32[2]{0:T(128)S(1)} %get-tuple-element.6), channel_id=1, replica_groups=mesh['dom'=32,'load'=8] {'dom'}, use_global_device_ids=true, to_apply=%region_1.0 | all-reduce | flops 4 | bytes 32 | tf_op jit(solution)/shard_map/psum | solution.py:43
  155.5 8.0 convolution_bitcast_fusion.5
  163.6 4.2 collective-permute-done.10
  167.9 5.0 collective-permute-done.11
  173.1 7.8 collective-permute-done.12
  180.9 12.3 collective-permute-start.13
  196.4 4.4 collective-permute-done.14
  206.0 60.2 %psum.65 = f32[2]{0:T(128)S(1)} all-reduce(f32[2]{0:T(128)S(1)} %get-tuple-element.29), channel_id=1, replica_groups=mesh['dom'=32,'load'=8] {'dom'}, use_global_device_ids=true, to_apply=%region_5.0 | all-reduce | flops 2 | bytes 16 | tf_op jit(solution)/shard_map/psum | solution.py:43
  266.6 8.0 convolution_bitcast_fusion.4
  279.0 5.0 collective-permute-done.16
  284.2 7.8 collective-permute-done.17
  292.1 11.9 collective-permute-start.18
  306.9 4.4 collective-permute-done.19
  316.5 62.2 %psum.66 = f32[2]{0:T(128)S(1)} all-reduce(f32[2]{0:T(128)S(1)} %get-tuple-element.31), channel_id=1, replica_groups=mesh['dom'=32,'load'=8] {'dom'}, use_global_device_ids=true, to_apply=%region_7.0 | all-reduce | flops 2 | bytes 16 | tf_op jit(solution)/shard_map/psum | solution.py:43
  379.1 8.0 convolution_bitcast_fusion.3
  387.2 4.2 collective-permute-done.20
  391.6 5.0 collective-permute-done.21
  396.8 7.9 collective-permute-done.22
  404.7 11.7 collective-permute-start.23
  419.3 4.4 collective-permute-done.24
  429.0 60.2 %psum.67 = f32[2]{0:T(128)S(1)} all-reduce(f32[2]{0:T(128)S(1)} %get-tuple-element.33), channel_id=1, replica_groups=mesh['dom'=32,'load'=8] {'dom'}, use_global_device_ids=true, to_apply=%region_9.0 | all-reduce | flops 2 | bytes 16 | tf_op jit(solution)/shard_map/psum | solution.py:43
  489.5 8.0 convolution_bitcast_fusion.2
  502.0 5.0 collective-permute-done.26
  507.1 7.8 collective-permute-done.27
  515.0 12.2 collective-permute-start.28
  530.3 4.4 collective-permute-done.29
  539.9 61.7 %psum.68 = f32[2]{0:T(128)S(1)} all-reduce(f32[2]{0:T(128)S(1)} %get-tuple-element.35), channel_id=1, replica_groups=mesh['dom'=32,'load'=8] {'dom'}, use_global_device_ids=true, to_apply=%region_11.0 | all-reduce | flops 2 | bytes 16 | tf_op jit(solution)/shard_map/psum | solution.py:43
  601.9 8.0 convolution_bitcast_fusion.1
  614.4 5.2 collective-permute-done.31
  619.8 7.8 collective-permute-done.32
  627.7 11.7 collective-permute-start.33
  642.3 4.4 collective-permute-done.34
  652.0 60.2 %psum.69 = f32[2]{0:T(128)S(1)} all-reduce(f32[2]{0:T(128)S(1)} %get-tuple-element.37), channel_id=1, replica_groups=mesh['dom'=32,'load'=8] {'dom'}, use_global_device_ids=true, to_apply=%region_13.0 | all-reduce | flops 2 | bytes 16 | tf_op jit(solution)/shard_map/psum | solution.py:43
  712.5 8.0 convolution_bitcast_fusion
  725.0 5.0 collective-permute-done.36
  730.1 7.8 collective-permute-done.37
  738.0 11.8 collective-permute-start.38
  752.7 4.4 collective-permute-done.39
  762.4 62.0 %psum.70 = f32[2]{0:T(128)S(1)} all-reduce(f32[2]{0:T(128)S(1)} %fusion.21), channel_id=1, replica_groups=mesh['dom'=32,'load'=8] {'dom'}, use_global_device_ids=true, to_apply=%region_15.0 | all-reduce | flops 2 | bytes 16 | tf_op jit(solution)/shard_map/psum | solution.py:43
  824.5 90.5 %gather_fusion.3 = f32[16384]{0:T(1024)S(1)} fusion(f32[1536]{0:T(1024)S(1)} %bitcast.279, s32[16384]{0:T(1024)S(1)} %get-tuple-element.39), kind=kCustom, calls=%fused_computation.3 | custom fusion | bytes 196608 | tf_op jit(solution)/shard_map/gather | solution.py:97
  915.0 90.5 %gather_fusion.1 = f32[16384]{0:T(1024)S(1)} fusion(f32[1536]{0:T(1024)S(1)} %bitcast.281, s32[16384]{0:T(1024)S(1)} %get-tuple-element.39), kind=kCustom, calls=%fused_computation.1 | custom fusion | bytes 196608 | tf_op jit(solution)/shard_map/gather | solution.py:98
  1005.6 90.5 %gather_fusion = f32[16384]{0:T(1024)S(1)} fusion(f32[1536]{0:T(1024)S(1)} %bitcast.282, s32[16384]{0:T(1024)S(1)} %get-tuple-element.40), kind=kCustom, calls=%fused_computation | custom fusion | bytes 196608 | tf_op jit(solution)/shard_map/gather | solution.py:98
  1096.1 90.5 %gather_fusion.2 = f32[16384]{0:T(1024)S(1)} fusion(f32[1536]{0:T(1024)S(1)} %bitcast.280, s32[16384]{0:T(1024)S(1)} %get-tuple-element.40), kind=kCustom, calls=%fused_computation.2 | custom fusion | bytes 196608 | tf_op jit(solution)/shard_map/gather | solution.py:97
  1188.0 68.5 %all-reduce.3.cloned.1.call-done = f32[16384]{0:T(1024)} async-done(((f32[16384]{0:T(1024)}), f32[16384]{0:T(1024)}) %all-reduce.3.cloned.1.call-update) | async-done | bytes 65552 | tf_op jit(solution)/shard_map/psum | solution.py:99
  (243 shorter events, 127.4 us)
Async XLA Ops:
  7.2 1249.2 %all-reduce.3.cloned.1.call-start = ((), (), s32[]{:S(2)}) async-start(), calls=%async_computation | async-start | bytes 131072 | tf_op jit(solution)/shard_map/psum | solution.py:99
  17.9 4.3 collective-permute-start
  22.2 5.4 collective-permute-start.1
  27.7 8.9 collective-permute-start.2
  36.6 3.9 collective-permute-start.3
  40.6 5.5 collective-permute-start.4
  57.6 4.2 collective-permute-start.5
  61.9 5.1 collective-permute-start.6
  67.1 8.9 collective-permute-start.7
  76.0 3.9 collective-permute-start.8
  79.9 5.5 collective-permute-start.9
  155.1 45.7 %copy-start.2 = (f32[5,12,128,128]{3,2,1,0:T(8,128)S(1)}, f32[5,12,128,128]{3,2,1,0:T(8,128)}, u32[]{:S(2)}) copy-start(f32[5,12,128,128]{3,2,1,0:T(8,128)} %param.14) | copy-start | bytes 11796484
  163.5 4.3 collective-permute-start.10
  167.8 5.1 collective-permute-start.11
  173.0 8.0 collective-permute-start.12
  180.9 14.1 %collective-permute-start.13 = (f32[2,2,12,128]{3,1,2,0:T(2,128)S(1)}, f32[2,2,12,128]{3,1,2,0:T(2,128)S(1)}, u32[]{:S(2)}, u32[]{:S(2)}) collective-permute-start(f32[2,2,12,128]{3,1,2,0:T(2,128)S(1)} %slice.305), channel_id=1, source_target_pairs={{0,64},{8,72},{16,80},{24,88},{32,96},{40,104},{48,112},{56,120},{... | collective-permute-start | bytes 73736 | tf_op jit(solution)/shard_map/ppermute | solution.py:14
  195.1 5.7 collective-permute-start.14
  266.2 45.1 %copy-start.3 = (f32[5,12,128,128]{3,2,1,0:T(8,128)S(1)}, f32[5,12,128,128]{3,2,1,0:T(8,128)}, u32[]{:S(2)}) copy-start(f32[5,12,128,128]{3,2,1,0:T(8,128)} %param.14) | copy-start | bytes 11796484
  274.6 4.3 collective-permute-start.15
  278.9 5.1 collective-permute-start.16
  284.1 8.0 collective-permute-start.17
  292.1 13.7 %collective-permute-start.18 = (f32[2,2,12,128]{3,1,2,0:T(2,128)S(1)}, f32[2,2,12,128]{3,1,2,0:T(2,128)S(1)}, u32[]{:S(2)}, u32[]{:S(2)}) collective-permute-start(f32[2,2,12,128]{3,1,2,0:T(2,128)S(1)} %slice.313), channel_id=1, source_target_pairs={{0,64},{8,72},{16,80},{24,88},{32,96},{40,104},{48,112},{56,120},{... | collective-permute-start | bytes 73736 | tf_op jit(solution)/shard_map/ppermute | solution.py:14
  305.9 5.5 collective-permute-start.19
  378.8 45.0 %copy-start.4 = (f32[5,12,128,128]{3,2,1,0:T(8,128)S(1)}, f32[5,12,128,128]{3,2,1,0:T(8,128)}, u32[]{:S(2)}) copy-start(f32[5,12,128,128]{3,2,1,0:T(8,128)} %param.14) | copy-start | bytes 11796484
  387.2 4.3 collective-permute-start.20
  391.5 5.1 collective-permute-start.21
  396.7 8.0 collective-permute-start.22
  404.7 13.5 %collective-permute-start.23 = (f32[2,2,12,128]{3,1,2,0:T(2,128)S(1)}, f32[2,2,12,128]{3,1,2,0:T(2,128)S(1)}, u32[]{:S(2)}, u32[]{:S(2)}) collective-permute-start(f32[2,2,12,128]{3,1,2,0:T(2,128)S(1)} %slice.321), channel_id=1, source_target_pairs={{0,64},{8,72},{16,80},{24,88},{32,96},{40,104},{48,112},{56,120},{... | collective-permute-start | bytes 73736 | tf_op jit(solution)/shard_map/ppermute | solution.py:14
  418.2 5.5 collective-permute-start.24
  489.2 45.5 %copy-start.5 = (f32[5,12,128,128]{3,2,1,0:T(8,128)S(1)}, f32[5,12,128,128]{3,2,1,0:T(8,128)}, u32[]{:S(2)}) copy-start(f32[5,12,128,128]{3,2,1,0:T(8,128)} %param.14) | copy-start | bytes 11796484
  497.5 4.3 collective-permute-start.25
  501.9 5.1 collective-permute-start.26
  507.0 8.0 collective-permute-start.27
  515.0 14.0 %collective-permute-start.28 = (f32[2,2,12,128]{3,1,2,0:T(2,128)S(1)}, f32[2,2,12,128]{3,1,2,0:T(2,128)S(1)}, u32[]{:S(2)}, u32[]{:S(2)}) collective-permute-start(f32[2,2,12,128]{3,1,2,0:T(2,128)S(1)} %slice.329), channel_id=1, source_target_pairs={{0,64},{8,72},{16,80},{24,88},{32,96},{40,104},{48,112},{56,120},{... | collective-permute-start | bytes 73736 | tf_op jit(solution)/shard_map/ppermute | solution.py:14
  529.0 5.7 collective-permute-start.29
  601.6 45.1 %copy-start.6 = (f32[5,12,128,128]{3,2,1,0:T(8,128)S(1)}, f32[5,12,128,128]{3,2,1,0:T(8,128)}, u32[]{:S(2)}) copy-start(f32[5,12,128,128]{3,2,1,0:T(8,128)} %param.14) | copy-start | bytes 11796484
  610.0 4.3 collective-permute-start.30
  614.3 5.4 collective-permute-start.31
  619.7 8.0 collective-permute-start.32
  627.7 13.5 %collective-permute-start.33 = (f32[2,2,12,128]{3,1,2,0:T(2,128)S(1)}, f32[2,2,12,128]{3,1,2,0:T(2,128)S(1)}, u32[]{:S(2)}, u32[]{:S(2)}) collective-permute-start(f32[2,2,12,128]{3,1,2,0:T(2,128)S(1)} %slice.337), channel_id=1, source_target_pairs={{0,64},{8,72},{16,80},{24,88},{32,96},{40,104},{48,112},{56,120},{... | collective-permute-start | bytes 73736 | tf_op jit(solution)/shard_map/ppermute | solution.py:14
  641.3 5.5 collective-permute-start.34
  646.7 75.6 %copy-start.12 = (s32[2,16384]{1,0:T(2,128)S(1)}, s32[2,16384]{1,0:T(2,128)}, u32[]{:S(2)}) copy-start(s32[2,16384]{1,0:T(2,128)} %param.16) | copy-start | bytes 393220
  712.2 44.9 %copy-start.7 = (f32[5,12,128,128]{3,2,1,0:T(8,128)S(1)}, f32[5,12,128,128]{3,2,1,0:T(8,128)}, u32[]{:S(2)}) copy-start(f32[5,12,128,128]{3,2,1,0:T(8,128)} %param.14) | copy-start | bytes 11796484
  720.6 4.3 collective-permute-start.35
  724.9 5.1 collective-permute-start.36
  730.0 8.0 collective-permute-start.37
  738.0 13.6 %collective-permute-start.38 = (f32[2,2,12,128]{3,1,2,0:T(2,128)S(1)}, f32[2,2,12,128]{3,1,2,0:T(2,128)S(1)}, u32[]{:S(2)}, u32[]{:S(2)}) collective-permute-start(f32[2,2,12,128]{3,1,2,0:T(2,128)S(1)} %slice.345), channel_id=1, source_target_pairs={{0,64},{8,72},{16,80},{24,88},{32,96},{40,104},{48,112},{56,120},{... | collective-permute-start | bytes 73736 | tf_op jit(solution)/shard_map/ppermute | solution.py:14
  751.6 5.5 collective-permute-start.39
  (8 other events, 248.9 us)
Sparse Core Ops, SparseCore 0:
  1187.5 68.9 all-reduce.2
where the time goes:
time: 1270 us; the launch traced here: 1260 us
  blocking collectives  431 us (34%)
  local copies, waits for them, and re-layouts  365 us (29%)
  waiting for transfers between devices  226 us (18%)
  matrix products  113 us (9%)
  starting transfers between devices  112 us (9%)
  between operations  15.9 us (1%)
    psum x7, blocking collectives, column_sums(): return lax.psum(jnp.sum(first * second, axis=(1, 2)), 'dom')  431 us
    gather x2, local copies, waits for them, and re-layouts, shards(): adj_diff = adjoint[:, strap_ends[0]] - adjoint[:, strap_ends[1]]  181 us
    gather x2, local copies, waits for them, and re-layouts, shards(): drop_diff = forward[:, strap_ends[0]] - forward[:, strap_ends[1]]  181 us
    ppermute x40, waiting for transfers between devices, swapped(): return lax.ppermute(value, axis, pairs)  157 us
    ppermute x40, starting transfers between devices, swapped(): return lax.ppermute(value, axis, pairs)  112 us
    psum x1, waiting for transfers between devices, shards(): strap_grad = lax.psum(-jnp.sum(adj_diff * drop_diff, axis=0), 'load')  68.5 us
    dot_general x8, matrix products, coarse_part(): jnp.einsum('ljmn,lrjn->lrjm', coupling, selected, precision=HIGHEST)  62.3 us
    dot_general x8, matrix products, coarse_part(): jnp.einsum('ljmn,lrjm->lrjn', coupling, group_sums, precision=HIGHEST)  27.5 us
  transfers between devices with their start and end apart: 41, of which 41 were waited for; matrix products, arithmetic and copies ran while one was open for 1% of the time, Pallas kernels for 0%

commit v1 on v0

--- a/solution.py
+++ b/solution.py
@@ -96,7 +96,7 @@
     adjoint = voltages[1]
     drop_diff = forward[:, strap_ends[0]] - forward[:, strap_ends[1]]
     adj_diff = adjoint[:, strap_ends[0]] - adjoint[:, strap_ends[1]]
-    strap_grad = lax.psum(-jnp.sum(adj_diff * drop_diff, axis=0), "load")
+    strap_grad = jnp.sum(lax.all_gather(-jnp.sum(adj_diff * drop_diff, axis=0), "load"), axis=0)
     return (voltages, strap_grad)
 
 

time: 1270 us -> 1210 us (0.953)
  waiting for transfers between devices: 226 us -> 157 us
  blocking collectives: 431 us -> 445 us
  between operations: 15.9 us -> 2.49 us
    psum x1 -> x0, waiting for transfers between devices: 68.5 us -> none  [shards(): strap_grad = lax.psum(-jnp.sum(adj_diff * drop_diff, axis=0), 'load')]
    all_gather x0 -> x1, blocking collectives: none -> 13.6 us  [shards(): lax.all_gather(-jnp.sum(adj_diff * drop_diff, axis=0), 'load')]
  transfers between devices with their start and end apart: 41 -> 40, of which waited for: 41 -> 40; matrix products, arithmetic and copies ran while one was open for 1% -> 1% of each run, Pallas kernels for 0% -> 0%
where the time goes in v1:
time: 1210 us; the launch traced here: 1200 us
  blocking collectives  445 us (37%)
  local copies, waits for them, and re-layouts  363 us (30%)
  waiting for transfers between devices  157 us (13%)
  matrix products  113 us (9%)
  starting transfers between devices  112 us (9%)
    psum x7, blocking collectives, column_sums(): return lax.psum(jnp.sum(first * second, axis=(1, 2)), 'dom')  431 us
    gather x2, local copies, waits for them, and re-layouts, shards(): drop_diff = forward[:, strap_ends[0]] - forward[:, strap_ends[1]]  181 us
    gather x2, local copies, waits for them, and re-layouts, shards(): adj_diff = adjoint[:, strap_ends[0]] - adjoint[:, strap_ends[1]]  181 us
    ppermute x40, waiting for transfers between devices, swapped(): return lax.ppermute(value, axis, pairs)  157 us
    ppermute x40, starting transfers between devices, swapped(): return lax.ppermute(value, axis, pairs)  112 us
    dot_general x8, matrix products, coarse_part(): jnp.einsum('ljmn,lrjn->lrjm', coupling, selected, precision=HIGHEST)  62.3 us
    dot_general x8, matrix products, coarse_part(): jnp.einsum('ljmn,lrjm->lrjn', coupling, group_sums, precision=HIGHEST)  27.5 us
  transfers between devices with their start and end apart: 40, of which 40 were waited for; matrix products, arithmetic and copies ran while one was open for 1% of the time, Pallas kernels for 0%

profile of v1, /device:TPU:2, one launch (start us, length us, event | category | flops | bytes accessed | tf_op | source)
XLA Modules:
  0.0 1195.4 jit_solution(9342061517297214624)
XLA Ops:
  3.4 7.9 convolution_bitcast_fusion.23
  21.1 7.0 collective-permute-start.2
  44.8 6.2 convolution_bitcast_fusion.21
  60.5 6.9 collective-permute-start.7
  84.1 64.4 %all-reduce = (f32[2]{0:T(128)S(1)}, f32[2]{0:T(128)S(1)}) all-reduce(f32[2]{0:T(128)S(1)} %get-tuple-element.11, f32[2]{0:T(128)S(1)} %get-tuple-element.10), channel_id=1, replica_groups=mesh['dom'=32,'load'=8] {'dom'}, use_global_device_ids=true, to_apply=%region_1.0 | all-reduce | flops 4 | bytes 32 | tf_op jit(solution)/shard_map/psum | solution.py:43
  148.9 8.0 convolution_bitcast_fusion.19
  157.0 4.2 collective-permute-done.10
  161.4 5.0 collective-permute-done.11
  166.5 7.8 collective-permute-done.12
  174.4 12.4 %collective-permute-start.13 = (f32[2,2,12,128]{3,1,2,0:T(2,128)S(1)}, f32[2,2,12,128]{3,1,2,0:T(2,128)S(1)}, u32[]{:S(2)}, u32[]{:S(2)}) collective-permute-start(f32[2,2,12,128]{3,1,2,0:T(2,128)S(1)} %slice.305), channel_id=1, source_target_pairs={{0,64},{8,72},{16,80},{24,88},{32,96},{40,104},{48,112},{56,120},{... | collective-permute-start | bytes 73736 | tf_op jit(solution)/shard_map/ppermute | solution.py:14
  189.8 4.4 collective-permute-done.14
  199.5 60.2 %psum.58 = f32[2]{0:T(128)S(1)} all-reduce(f32[2]{0:T(128)S(1)} %get-tuple-element.33), channel_id=1, replica_groups=mesh['dom'=32,'load'=8] {'dom'}, use_global_device_ids=true, to_apply=%region_5.0 | all-reduce | flops 2 | bytes 16 | tf_op jit(solution)/shard_map/psum | solution.py:43
  260.0 8.0 convolution_bitcast_fusion.17
  272.5 5.0 collective-permute-done.16
  277.6 7.8 collective-permute-done.17
  285.5 11.9 collective-permute-start.18
  300.3 4.4 collective-permute-done.19
  310.0 62.2 %psum.59 = f32[2]{0:T(128)S(1)} all-reduce(f32[2]{0:T(128)S(1)} %get-tuple-element.35), channel_id=1, replica_groups=mesh['dom'=32,'load'=8] {'dom'}, use_global_device_ids=true, to_apply=%region_7.0 | all-reduce | flops 2 | bytes 16 | tf_op jit(solution)/shard_map/psum | solution.py:43
  372.5 8.0 convolution_bitcast_fusion.15
  380.6 4.3 collective-permute-done.20
  385.0 5.0 collective-permute-done.21
  390.2 7.9 collective-permute-done.22
  398.1 11.7 collective-permute-start.23
  412.7 4.4 collective-permute-done.24
  422.4 60.2 %psum.60 = f32[2]{0:T(128)S(1)} all-reduce(f32[2]{0:T(128)S(1)} %get-tuple-element.37), channel_id=1, replica_groups=mesh['dom'=32,'load'=8] {'dom'}, use_global_device_ids=true, to_apply=%region_9.0 | all-reduce | flops 2 | bytes 16 | tf_op jit(solution)/shard_map/psum | solution.py:43
  482.9 8.0 convolution_bitcast_fusion.13
  495.4 5.0 collective-permute-done.26
  500.5 7.8 collective-permute-done.27
  508.4 12.2 %collective-permute-start.28 = (f32[2,2,12,128]{3,1,2,0:T(2,128)S(1)}, f32[2,2,12,128]{3,1,2,0:T(2,128)S(1)}, u32[]{:S(2)}, u32[]{:S(2)}) collective-permute-start(f32[2,2,12,128]{3,1,2,0:T(2,128)S(1)} %slice.329), channel_id=1, source_target_pairs={{0,64},{8,72},{16,80},{24,88},{32,96},{40,104},{48,112},{56,120},{... | collective-permute-start | bytes 73736 | tf_op jit(solution)/shard_map/ppermute | solution.py:14
  523.7 4.4 collective-permute-done.29
  533.3 61.7 %psum.61 = f32[2]{0:T(128)S(1)} all-reduce(f32[2]{0:T(128)S(1)} %get-tuple-element.39), channel_id=1, replica_groups=mesh['dom'=32,'load'=8] {'dom'}, use_global_device_ids=true, to_apply=%region_11.0 | all-reduce | flops 2 | bytes 16 | tf_op jit(solution)/shard_map/psum | solution.py:43
  595.3 8.0 convolution_bitcast_fusion.11
  607.8 5.2 collective-permute-done.31
  613.2 7.8 collective-permute-done.32
  621.1 11.7 collective-permute-start.33
  635.7 4.4 collective-permute-done.34
  645.4 60.2 %psum.62 = f32[2]{0:T(128)S(1)} all-reduce(f32[2]{0:T(128)S(1)} %get-tuple-element.41), channel_id=1, replica_groups=mesh['dom'=32,'load'=8] {'dom'}, use_global_device_ids=true, to_apply=%region_13.0 | all-reduce | flops 2 | bytes 16 | tf_op jit(solution)/shard_map/psum | solution.py:43
  706.0 8.0 convolution_bitcast_fusion.9
  718.4 5.0 collective-permute-done.36
  723.5 7.8 collective-permute-done.37
  731.4 11.8 collective-permute-start.38
  746.1 4.4 collective-permute-done.39
  755.8 62.0 %psum.63 = f32[2]{0:T(128)S(1)} all-reduce(f32[2]{0:T(128)S(1)} %fusion.21), channel_id=1, replica_groups=mesh['dom'=32,'load'=8] {'dom'}, use_global_device_ids=true, to_apply=%region_15.0 | all-reduce | flops 2 | bytes 16 | tf_op jit(solution)/shard_map/psum | solution.py:43
  817.9 90.5 %gather_fusion.3 = f32[16384]{0:T(1024)S(1)} fusion(f32[1536]{0:T(1024)S(1)} %bitcast.270, s32[16384]{0:T(1024)S(1)} %get-tuple-element.43), kind=kCustom, calls=%fused_computation.3 | custom fusion | bytes 196608 | tf_op jit(solution)/shard_map/gather | solution.py:97
  908.5 90.5 %gather_fusion.1 = f32[16384]{0:T(1024)S(1)} fusion(f32[1536]{0:T(1024)S(1)} %bitcast.272, s32[16384]{0:T(1024)S(1)} %get-tuple-element.43), kind=kCustom, calls=%fused_computation.1 | custom fusion | bytes 196608 | tf_op jit(solution)/shard_map/gather | solution.py:98
  999.0 90.5 %gather_fusion = f32[16384]{0:T(1024)S(1)} fusion(f32[1536]{0:T(1024)S(1)} %bitcast.273, s32[16384]{0:T(1024)S(1)} %get-tuple-element.44), kind=kCustom, calls=%fused_computation | custom fusion | bytes 196608 | tf_op jit(solution)/shard_map/gather | solution.py:98
  1089.5 90.5 %gather_fusion.2 = f32[16384]{0:T(1024)S(1)} fusion(f32[1536]{0:T(1024)S(1)} %bitcast.271, s32[16384]{0:T(1024)S(1)} %get-tuple-element.44), kind=kCustom, calls=%fused_computation.2 | custom fusion | bytes 196608 | tf_op jit(solution)/shard_map/gather | solution.py:97
  1180.7 13.6 %all-gather = f32[131072]{0:T(1024)S(1)} all-gather(f32[16384]{0:T(1024)S(1)} %multiply_negate_fusion), channel_id=2, replica_groups=mesh['dom'=32,'load'=8] {'load'}, dimensions={0}, use_global_device_ids=true | all-gather | bytes 589824 | tf_op jit(solution)/shard_map/all_gather | solution.py:99
  (242 shorter events, 126.2 us)
Async XLA Ops:
  3.4 39.5 %copy-start.9 = (s32[5,12]{1,0:T(8,128)S(1)}, s32[5,12]{1,0:T(8,128)}, u32[]{:S(2)}) copy-start(s32[5,12]{1,0:T(8,128)} %param.15) | copy-start | bytes 724
  11.3 4.3 collective-permute-start
  15.6 5.4 collective-permute-start.1
  21.1 8.9 collective-permute-start.2
  30.0 3.9 collective-permute-start.3
  34.0 5.5 collective-permute-start.4
  51.0 4.2 collective-permute-start.5
  55.3 5.1 collective-permute-start.6
  60.5 8.9 collective-permute-start.7
  69.4 3.9 collective-permute-start.8
  73.4 5.5 collective-permute-start.9
  148.6 45.7 %copy-start.2 = (f32[5,12,128,128]{3,2,1,0:T(8,128)S(1)}, f32[5,12,128,128]{3,2,1,0:T(8,128)}, u32[]{:S(2)}) copy-start(f32[5,12,128,128]{3,2,1,0:T(8,128)} %param.14) | copy-start | bytes 11796484
  156.9 4.3 collective-permute-start.10
  161.2 5.1 collective-permute-start.11
  166.4 8.0 collective-permute-start.12
  174.4 14.2 %collective-permute-start.13 = (f32[2,2,12,128]{3,1,2,0:T(2,128)S(1)}, f32[2,2,12,128]{3,1,2,0:T(2,128)S(1)}, u32[]{:S(2)}, u32[]{:S(2)}) collective-permute-start(f32[2,2,12,128]{3,1,2,0:T(2,128)S(1)} %slice.305), channel_id=1, source_target_pairs={{0,64},{8,72},{16,80},{24,88},{32,96},{40,104},{48,112},{56,120},{... | collective-permute-start | bytes 73736 | tf_op jit(solution)/shard_map/ppermute | solution.py:14
  188.6 5.7 collective-permute-start.14
  259.7 45.1 %copy-start.3 = (f32[5,12,128,128]{3,2,1,0:T(8,128)S(1)}, f32[5,12,128,128]{3,2,1,0:T(8,128)}, u32[]{:S(2)}) copy-start(f32[5,12,128,128]{3,2,1,0:T(8,128)} %param.14) | copy-start | bytes 11796484
  268.0 4.3 collective-permute-start.15
  272.3 5.1 collective-permute-start.16
  277.5 8.0 collective-permute-start.17
  285.5 13.7 %collective-permute-start.18 = (f32[2,2,12,128]{3,1,2,0:T(2,128)S(1)}, f32[2,2,12,128]{3,1,2,0:T(2,128)S(1)}, u32[]{:S(2)}, u32[]{:S(2)}) collective-permute-start(f32[2,2,12,128]{3,1,2,0:T(2,128)S(1)} %slice.313), channel_id=1, source_target_pairs={{0,64},{8,72},{16,80},{24,88},{32,96},{40,104},{48,112},{56,120},{... | collective-permute-start | bytes 73736 | tf_op jit(solution)/shard_map/ppermute | solution.py:14
  299.3 5.5 collective-permute-start.19
  372.2 45.0 %copy-start.4 = (f32[5,12,128,128]{3,2,1,0:T(8,128)S(1)}, f32[5,12,128,128]{3,2,1,0:T(8,128)}, u32[]{:S(2)}) copy-start(f32[5,12,128,128]{3,2,1,0:T(8,128)} %param.14) | copy-start | bytes 11796484
  380.6 4.3 collective-permute-start.20
  384.9 5.1 collective-permute-start.21
  390.1 8.0 collective-permute-start.22
  398.1 13.5 %collective-permute-start.23 = (f32[2,2,12,128]{3,1,2,0:T(2,128)S(1)}, f32[2,2,12,128]{3,1,2,0:T(2,128)S(1)}, u32[]{:S(2)}, u32[]{:S(2)}) collective-permute-start(f32[2,2,12,128]{3,1,2,0:T(2,128)S(1)} %slice.321), channel_id=1, source_target_pairs={{0,64},{8,72},{16,80},{24,88},{32,96},{40,104},{48,112},{56,120},{... | collective-permute-start | bytes 73736 | tf_op jit(solution)/shard_map/ppermute | solution.py:14
  411.7 5.5 collective-permute-start.24
  482.6 45.5 %copy-start.5 = (f32[5,12,128,128]{3,2,1,0:T(8,128)S(1)}, f32[5,12,128,128]{3,2,1,0:T(8,128)}, u32[]{:S(2)}) copy-start(f32[5,12,128,128]{3,2,1,0:T(8,128)} %param.14) | copy-start | bytes 11796484
  491.0 4.3 collective-permute-start.25
  495.3 5.1 collective-permute-start.26
  500.4 8.0 collective-permute-start.27
  508.4 14.0 %collective-permute-start.28 = (f32[2,2,12,128]{3,1,2,0:T(2,128)S(1)}, f32[2,2,12,128]{3,1,2,0:T(2,128)S(1)}, u32[]{:S(2)}, u32[]{:S(2)}) collective-permute-start(f32[2,2,12,128]{3,1,2,0:T(2,128)S(1)} %slice.329), channel_id=1, source_target_pairs={{0,64},{8,72},{16,80},{24,88},{32,96},{40,104},{48,112},{56,120},{... | collective-permute-start | bytes 73736 | tf_op jit(solution)/shard_map/ppermute | solution.py:14
  522.4 5.7 collective-permute-start.29
  595.0 45.1 %copy-start.6 = (f32[5,12,128,128]{3,2,1,0:T(8,128)S(1)}, f32[5,12,128,128]{3,2,1,0:T(8,128)}, u32[]{:S(2)}) copy-start(f32[5,12,128,128]{3,2,1,0:T(8,128)} %param.14) | copy-start | bytes 11796484
  603.4 4.3 collective-permute-start.30
  607.7 5.4 collective-permute-start.31
  613.1 8.0 collective-permute-start.32
  621.1 13.6 %collective-permute-start.33 = (f32[2,2,12,128]{3,1,2,0:T(2,128)S(1)}, f32[2,2,12,128]{3,1,2,0:T(2,128)S(1)}, u32[]{:S(2)}, u32[]{:S(2)}) collective-permute-start(f32[2,2,12,128]{3,1,2,0:T(2,128)S(1)} %slice.337), channel_id=1, source_target_pairs={{0,64},{8,72},{16,80},{24,88},{32,96},{40,104},{48,112},{56,120},{... | collective-permute-start | bytes 73736 | tf_op jit(solution)/shard_map/ppermute | solution.py:14
  634.7 5.5 collective-permute-start.34
  640.2 75.6 %copy-start.12 = (s32[2,16384]{1,0:T(2,128)S(1)}, s32[2,16384]{1,0:T(2,128)}, u32[]{:S(2)}) copy-start(s32[2,16384]{1,0:T(2,128)} %param.16) | copy-start | bytes 393220
  705.6 44.9 %copy-start.7 = (f32[5,12,128,128]{3,2,1,0:T(8,128)S(1)}, f32[5,12,128,128]{3,2,1,0:T(8,128)}, u32[]{:S(2)}) copy-start(f32[5,12,128,128]{3,2,1,0:T(8,128)} %param.14) | copy-start | bytes 11796484
  714.0 4.3 collective-permute-start.35
  718.3 5.1 collective-permute-start.36
  723.4 8.0 collective-permute-start.37
  731.4 13.6 %collective-permute-start.38 = (f32[2,2,12,128]{3,1,2,0:T(2,128)S(1)}, f32[2,2,12,128]{3,1,2,0:T(2,128)S(1)}, u32[]{:S(2)}, u32[]{:S(2)}) collective-permute-start(f32[2,2,12,128]{3,1,2,0:T(2,128)S(1)} %slice.345), channel_id=1, source_target_pairs={{0,64},{8,72},{16,80},{24,88},{32,96},{40,104},{48,112},{56,120},{... | collective-permute-start | bytes 73736 | tf_op jit(solution)/shard_map/ppermute | solution.py:14
  745.0 5.5 collective-permute-start.39
  (7 other events, 209.2 us)
